TPU v7x, 32 devices: a whole 2x2x4 slice. The times are simulated.
32 devices in a mesh: dev: 32 (over z, y, x, core).
Axes of the slice: x: 2, y: 2, z: 4, core: 2. Of those that a mesh axis runs over, the one named last changes fastest.
Arguments:
- density_rows: bfloat16 [24576, 3840], P('dev')
- center_x: float32 [24576], replicated, may hold values from -0.25 to 1.25
- center_y: float32 [24576], replicated, may hold values from 0 to 1
- center_z: float32 [24576], replicated, may hold values from 0 to 1
- exponent: float32 [24576], replicated, may hold values from 0.5 to 150
- brick_blocks: int32 [32, 8], replicated, may hold values from 0 to 191, as said below
Outputs:
- potential: float32 [32, 4096], P('dev')
- ham_rows: float32 [24576, 3840], P('dev')
Inputs may be any that keep to these rules, and one draw needn't show every extreme that they name: `brick_blocks`: brick b belongs to device d = b. Its 8 entries are distinct blocks; 4 of them are owned by one of the devices d - 1, d, d + 1 (cyclically) and 2 by each of the other two, where block I is owned by device I // 6. Which of the three owns 4 changes from brick to brick. Blocks 0 and 191 touch brick 0.
All inputs are finite; a program needn't handle non-finite values.
Results may differ from a plain program's by a relative error of at most 0.00041.
Values may be sent and summed in bfloat16 or wider, within the bound.
A program may use at most 128 MiB of HBM per device.

v0:
```python
import functools
import math

import jax
import jax.numpy as jnp
from jax import lax
from jax.experimental import pallas as pl
from jax.experimental.pallas import tpu as pltpu
from jax.sharding import PartitionSpec as P

FB = 128
KB = 8
CAP = 4
BLK_DEV = 6
SIDE = 16
LAYER = SIDE * SIDE
CELLS = SIDE * SIDE * SIDE
COLS = 5 * BLK_DEV * FB
ROWS = BLK_DEV * FB
HALF = 64
VMEM_BYTES = 60 * 1024 * 1024

omega = 2.0 / 3.0
four_pi = 4.0 * math.pi
slater = (3.0 / math.pi) ** (1.0 / 3.0)
f32 = jnp.float32
bf16 = jnp.bfloat16


def wrapped(distance):
    moved = distance + 0.5
    return (moved - jnp.floor(moved)) - 0.5


def fill_orbitals(brick, devices, bb_ref, param_refs, rows_ref, orb_ref):
    point = (lax.broadcasted_iota(jnp.int32, (SIDE, FB), 0).astype(f32) + 0.5) / SIDE

    def one_block(a, carry):
        block = bb_ref[brick, a]
        owner = block // BLK_DEV
        offset = (lax.rem(brick - owner + 1 + devices, devices) - 1).astype(f32)
        mid_x, mid_y, mid_z, rate = [ref[pl.ds(block, 1), :] for ref in param_refs]
        rate = -rate
        along_x = (offset + point) - mid_x
        along_y = wrapped(point - mid_y)
        along_z = wrapped(point - mid_z)
        factor_x = jnp.exp(rate * along_x * along_x).T
        factor_y = jnp.exp(rate * along_y * along_y)
        factor_z = jnp.exp(rate * along_z * along_z)
        for j in range(SIDE):
            rows_ref[j * SIDE : (j + 1) * SIDE, :] = factor_y[j : j + 1] * factor_z
        factor_yz = rows_ref[...].T
        for h in range(FB // HALF):
            part = slice(h * HALF, (h + 1) * HALF)
            start = pl.multiple_of(a * FB + h * HALF, HALF)
            for i in range(SIDE):
                orb_ref[pl.ds(start, HALF), i * LAYER : (i + 1) * LAYER] = (
                    factor_x[part, i : i + 1] * factor_yz[part]
                ).astype(bf16)
        return carry

    lax.fori_loop(0, KB, one_block, 0)


def find_slots(brick, me, bb_ref, sel_ref):
    for k in range(CAP):
        sel_ref[k] = 0
    count = jnp.int32(0)
    for a in range(KB):
        mine = bb_ref[brick, a] // BLK_DEV == me

        @pl.when(mine)
        def _():
            sel_ref[count] = a

        count = count + mine.astype(jnp.int32)
    return count


def column_block(brick, c, me, devices, bb_ref):
    block = bb_ref[brick, c]
    owner = block // BLK_DEV
    return lax.rem(owner - me + 2 + devices, devices) * BLK_DEV + (block - owner * BLK_DEV)


def row_block(brick, slot, bb_ref):
    return lax.rem(bb_ref[brick, slot], BLK_DEV)


def density_kernel(
    devices,
    bb_ref,
    rows_hbm,
    cx,
    cy,
    cz,
    ex,
    pd_ref,
    sum_ref,
    orb_hbm,
    rows_vmem,
    orb_all,
    mat_ref,
    tmp_ref,
    sel_ref,
    sem,
    orb_sem,
):
    me = lax.axis_index("dev")
    load = pltpu.make_async_copy(rows_hbm, rows_vmem, sem)
    load.start()

    def keep(t):
        return pltpu.make_async_copy(orb_all.at[t], orb_hbm.at[t], orb_sem.at[t])

    def one_brick(t, carry):
        brick = lax.rem(me + t - 1 + devices, devices)
        orb_ref = orb_all.at[t]
        fill_orbitals(brick, devices, bb_ref, (cx, cy, cz, ex), tmp_ref, orb_ref)
        keep(t).start()
        count = find_slots(brick, me, bb_ref, sel_ref)

        @pl.when(t == 0)
        def _():
            load.wait()

        for k in range(CAP):
            here = pl.ds(k * FB, FB)

            @pl.when(k < count)
            def _():
                row = pl.multiple_of(row_block(brick, sel_ref[k], bb_ref) * FB, FB)
                for c in range(KB):
                    col = pl.multiple_of(column_block(brick, c, me, devices, bb_ref) * FB, FB)
                    mat_ref[here, c * FB : (c + 1) * FB] = rows_vmem[pl.ds(row, FB), pl.ds(col, FB)]

            @pl.when(k >= count)
            def _():
                mat_ref[here, :] = jnp.zeros((FB, KB * FB), bf16)

        def one_chunk(j, inner):
            chunk = pl.ds(pl.multiple_of(j * 2 * LAYER, 2 * LAYER), 2 * LAYER)
            applied = jnp.dot(mat_ref[...], orb_ref[:, chunk], preferred_element_type=f32)
            total = jnp.zeros((1, 2 * LAYER), f32)
            for k in range(CAP):
                row = pl.multiple_of(sel_ref[k] * FB, FB)
                own = orb_ref[pl.ds(row, FB), chunk].astype(f32)
                total = total + jnp.sum(own * applied[k * FB : (k + 1) * FB], axis=0, keepdims=True)
            pd_ref[t, pl.ds(2 * j, 1), :] = total[:, :LAYER]
            pd_ref[t, pl.ds(2 * j + 1, 1), :] = total[:, LAYER:]
            return inner

        lax.fori_loop(0, SIDE // 2, one_chunk, 0)
        return carry

    lax.fori_loop(0, 3, one_brick, 0)
    layer = jnp.sum(pd_ref[0] + pd_ref[1] + pd_ref[2], axis=0, keepdims=True)
    sum_ref[0] = layer[:, :FB] + layer[:, FB:]
    for t in range(3):
        keep(t).wait()


def potential_kernel(
    devices, pd_ref, sum_ref, out_ref, left1, right1, left2, right2, left3, right3, sums, send_sem, recv_sem, all_sem
):
    me = lax.axis_index("dev")
    barrier = pltpu.get_barrier_semaphore()

    def at(step):
        return lax.rem(me + step + devices, devices)

    def greet(k, carry):
        pl.semaphore_signal(
            barrier, inc=1, device_id=(lax.rem(me + k, devices),), device_id_type=pl.DeviceIdType.MESH
        )
        return carry

    lax.fori_loop(1, devices, greet, 0)
    pl.semaphore_wait(barrier, devices - 1)

    def to_all(k):
        return pltpu.make_async_remote_copy(
            src_ref=sum_ref.at[0],
            dst_ref=sums.at[k - 1],
            send_sem=all_sem.at[0],
            recv_sem=all_sem.at[1],
            device_id=(lax.rem(me + k, devices),),
            device_id_type=pl.DeviceIdType.MESH,
        )

    def start_sum(k, carry):
        to_all(k).start()
        return carry

    plan = (
        (pd_ref, left1, 1),
        (pd_ref, right1, -1),
        (pd_ref.at[pl.ds(1, 2)], left2, 2),
        (pd_ref.at[pl.ds(0, 2)], right2, -2),
        (pd_ref.at[2, pl.ds(8, 8)], left3, 3),
        (pd_ref.at[0, pl.ds(0, 8)], right3, -3),
    )
    copies = [
        pltpu.make_async_remote_copy(
            src_ref=src,
            dst_ref=dst,
            send_sem=send_sem.at[q],
            recv_sem=recv_sem.at[q],
            device_id=(at(step),),
            device_id_type=pl.DeviceIdType.MESH,
        )
        for q, (src, dst, step) in enumerate(plan)
    ]
    lax.fori_loop(1, devices, start_sum, 0)
    for copy in copies:
        copy.start()
    for copy in copies:
        copy.wait()
    pltpu.make_async_copy(sums, sums, all_sem.at[0]).wait()
    pltpu.make_async_copy(sums, sums, all_sem.at[1]).wait()

    total = jnp.sum(sums[...], axis=0) + sum_ref[0]
    average = jnp.sum(total, axis=1, keepdims=True) / (devices * CELLS)
    scale = omega * four_pi / 6.0
    here = pd_ref[1] + left1[2] + right1[0]
    behind = left1[1] + left2[1] + pd_ref[0]
    ahead = right1[1] + right2[0] + pd_ref[2]
    far_behind = (left2[0, 8:] + left3[...] + left1[0, 8:])[7:]
    far_ahead = (right2[1, :8] + right3[...] + right1[2, :8])[:1]
    lane = lax.broadcasted_iota(jnp.int32, (SIDE, LAYER), 1) % SIDE
    row = lax.broadcasted_iota(jnp.int32, (SIDE, LAYER), 0)
    cases = (
        (behind, far_behind, here[:1]),
        (here, behind[SIDE - 1 :], ahead[:1]),
        (ahead, here[SIDE - 1 :], far_ahead),
    )

    def moved(x, steps, axis):
        return pltpu.roll(x, steps % x.shape[axis], axis)

    for t, (density, before, after) in enumerate(cases):
        source = density - average
        one = scale * source
        up = jnp.where(row == 0, scale * (before - average), moved(one, 1, 0))
        down = jnp.where(row == SIDE - 1, scale * (after - average), moved(one, -1, 0))
        beside = up + down + moved(one, SIDE, 1) + moved(one, -SIDE, 1)
        beside = beside + jnp.where(lane == 0, moved(one, 1 - SIDE, 1), moved(one, 1, 1))
        beside = beside + jnp.where(lane == SIDE - 1, moved(one, SIDE - 1, 1), moved(one, -1, 1))
        two = one + omega * ((four_pi * source + beside) / 6.0 - one)
        size = jnp.abs(density)
        safe = jnp.where(size > 0.0, size, 1.0)
        root = jnp.exp(jnp.log(safe) / 3.0)
        root = root - (root - safe / (root * root)) / 3.0
        root = jnp.where(size > 0.0, root, 0.0)
        root = jnp.where(density < 0.0, -root, root)
        out_ref[t] = two - slater * root


def ham_kernel(devices, bb_ref, pot_ref, orb_hbm, out_hbm, acc_ref, orb_all, wei_ref, sel_ref, sem, orb_sem):
    me = lax.axis_index("dev")

    def fetch(t):
        return pltpu.make_async_copy(orb_hbm.at[t], orb_all.at[t], orb_sem.at[t])

    for t in range(3):
        fetch(t).start()

    def clear(r, carry):
        acc_ref[pl.ds(pl.multiple_of(r * 64, 64), 64), :] = jnp.zeros((64, COLS), f32)
        return carry

    lax.fori_loop(0, ROWS // 64, clear, 0)

    def one_brick(t, carry):
        brick = lax.rem(me + t - 1 + devices, devices)
        orb_ref = orb_all.at[t]
        count = find_slots(brick, me, bb_ref, sel_ref)
        fetch(t).wait()

        def weigh(k, inner):
            source = pl.multiple_of(sel_ref[k] * FB, FB)
            target = pl.multiple_of(k * FB, FB)
            for i in range(SIDE):
                cells = slice(i * LAYER, (i + 1) * LAYER)
                wei_ref[pl.ds(target, FB), cells] = (
                    orb_ref[pl.ds(source, FB), cells].astype(f32) * pot_ref[t, i : i + 1, :]
                ).astype(bf16)
            return inner

        lax.fori_loop(0, CAP, weigh, 0)

        def one_pair(q, inner):
            part = orb_ref[pl.ds(pl.multiple_of(q * 2 * FB, 2 * FB), 2 * FB), :]
            tile = lax.dot_general(
                wei_ref[...], part, (((1,), (1,)), ((), ())), preferred_element_type=f32
            ) * (64.0 / CELLS)
            for k in range(CAP):

                @pl.when(k < count)
                def _():
                    row = pl.multiple_of(row_block(brick, sel_ref[k], bb_ref) * FB, FB)
                    for c in range(2):
                        col = pl.multiple_of(column_block(brick, 2 * q + c, me, devices, bb_ref) * FB, FB)
                        acc_ref[pl.ds(row, FB), pl.ds(col, FB)] += tile[
                            k * FB : (k + 1) * FB, c * FB : (c + 1) * FB
                        ]

            return inner

        lax.fori_loop(0, KB // 2, one_pair, 0)
        return carry

    lax.fori_loop(0, 3, one_brick, 0)
    store = pltpu.make_async_copy(acc_ref, out_hbm, sem)
    store.start()
    store.wait()


def local(devices, density_rows, center_x, center_y, center_z, exponent, brick_blocks):
    params = [x.reshape(-1, FB) for x in (center_x, center_y, center_z, exponent)]
    vmem = pl.BlockSpec(memory_space=pltpu.VMEM)
    smem = pl.BlockSpec(memory_space=pltpu.SMEM)
    anywhere = pl.BlockSpec(memory_space=pl.ANY)
    grid = (3, SIDE, LAYER)
    partial, sums, orbitals = pl.pallas_call(
        functools.partial(density_kernel, devices),
        out_shape=(
            jax.ShapeDtypeStruct(grid, f32),
            jax.ShapeDtypeStruct((1, 1, FB), f32),
            jax.ShapeDtypeStruct((3, KB * FB, CELLS), bf16),
        ),
        in_specs=[smem, anywhere] + [vmem] * 4,
        out_specs=(vmem, vmem, anywhere),
        scratch_shapes=[
            pltpu.VMEM((ROWS, COLS), bf16),
            pltpu.VMEM((3, KB * FB, CELLS), bf16),
            pltpu.VMEM((CAP * FB, KB * FB), bf16),
            pltpu.VMEM((LAYER, FB), f32),
            pltpu.SMEM((CAP,), jnp.int32),
            pltpu.SemaphoreType.DMA,
            pltpu.SemaphoreType.DMA((3,)),
        ],
        compiler_params=pltpu.CompilerParams(vmem_limit_bytes=VMEM_BYTES),
        name="partial_density",
    )(brick_blocks, density_rows, *params)
    potentials = pl.pallas_call(
        functools.partial(potential_kernel, devices),
        out_shape=jax.ShapeDtypeStruct(grid, f32),
        in_specs=[vmem, vmem],
        out_specs=vmem,
        scratch_shapes=[
            pltpu.VMEM((3, SIDE, LAYER), f32),
            pltpu.VMEM((3, SIDE, LAYER), f32),
            pltpu.VMEM((2, SIDE, LAYER), f32),
            pltpu.VMEM((2, SIDE, LAYER), f32),
            pltpu.VMEM((8, LAYER), f32),
            pltpu.VMEM((8, LAYER), f32),
            pltpu.VMEM((devices - 1, 1, FB), f32),
            pltpu.SemaphoreType.DMA((6,)),
            pltpu.SemaphoreType.DMA((6,)),
            pltpu.SemaphoreType.DMA((2,)),
        ],
        compiler_params=pltpu.CompilerParams(collective_id=0, has_side_effects=True),
        name="exchange_potential",
    )(partial, sums)
    ham = pl.pallas_call(
        functools.partial(ham_kernel, devices),
        out_shape=jax.ShapeDtypeStruct((ROWS, COLS), f32),
        in_specs=[smem, vmem, anywhere],
        out_specs=anywhere,
        scratch_shapes=[
            pltpu.VMEM((ROWS, COLS), f32),
            pltpu.VMEM((3, KB * FB, CELLS), bf16),
            pltpu.VMEM((CAP * FB, CELLS), bf16),
            pltpu.SMEM((CAP,), jnp.int32),
            pltpu.SemaphoreType.DMA,
            pltpu.SemaphoreType.DMA((3,)),
        ],
        compiler_params=pltpu.CompilerParams(vmem_limit_bytes=VMEM_BYTES),
        name="ham_rows",
    )(brick_blocks, potentials, orbitals)
    return potentials[1].reshape(1, CELLS), ham


def solution(mesh):
    placed = (P("dev", None), P(), P(), P(), P(), P())
    return jax.shard_map(
        functools.partial(local, mesh.shape["dev"]),
        mesh=mesh,
        in_specs=placed,
        out_specs=(P("dev", None), P("dev", None)),
        check_vma=False,
    )
```

profile of v0, /device:TPU:0, one launch (start us, length us, event | category | flops | bytes accessed | tf_op | source)
XLA Modules:
  0.0 78.0 jit_solution(9135586207155241165)
XLA Ops:
  0.6 1.4 %copy.8.bb_ref = s32[32,8]{1,0:T(8,128)} copy(s32[32,8]{0,1:T(8,128)} %param.11) | data formatting | bytes 2048 | tf_op args[5]
  2.0 33.5 %partial_density.1 = (f32[3,16,256]{2,1,0:T(8,128)}, f32[1,1,128]{2,1,0:T(1,128)}, bf16[3,1024,4096]{2,1,0:T(8,128)(2,1)}) custom-call(s32[32,8]{1,0:T(8,128)} %copy.8.bb_ref, bf16[768,3840]{1,0:T(8,128)(2,1)} %rows_hbm.1, f32[192,128]{1,0:T(8,128)} %bitcast.7, f32[192,128]{1,0:T(8,128)} %bitcast.8, f32[192,128]{1,0:T(8,128)} %bitcast.9, f32[192,128]{1,0:T(8,128)} %bitcast.10), custom_call_target="tpu_custom_call" | custom-call | tf_op jit(solution)/shard_map/partial_density/pallas_call | solution.py:325
  35.5 13.3 %exchange_potential.1.pot_ref = f32[3,16,256]{2,1,0:T(8,128)} custom-call(f32[3,16,256]{2,1,0:T(8,128)} %get-tuple-element.5.pd_ref, f32[1,1,128]{2,1,0:T(1,128)} %get-tuple-element.6.sum_ref), custom_call_target="tpu_custom_call" | custom-call | tf_op jit(solution)/shard_map/exchange_potential/pallas_call | solution.py:346
  48.9 27.8 %ham_rows.1 = f32[768,3840]{1,0:T(8,128)} custom-call(s32[32,8]{1,0:T(8,128)} %copy.8.bb_ref, f32[3,16,256]{2,1,0:T(8,128)} %exchange_potential.1.pot_ref, bf16[3,1024,4096]{2,1,0:T(8,128)(2,1)} %get-tuple-element.7.orb_hbm), custom_call_target="tpu_custom_call" | custom-call | tf_op jit(solution)/shard_map/ham_rows/pallas_call | solution.py:366
  76.7 0.7 slice_bitcast_fusion
  77.4 0.6 copy.10
where the time goes:
time: 78.4 us; the launch traced here: 78 us
  Pallas kernels  74.6 us (95%)
  local copies, waits for them, and re-layouts  2.71 us (3%)
    pallas_call x1, Pallas kernels, local(): pl.pallas_call(functools.partial(density_kernel, devices), out_shape=(jax...  33.5 us
    pallas_call x1, Pallas kernels, local(): pl.pallas_call(functools.partial(ham_kernel, devices), out_shape=jax.Shap...  27.8 us
    pallas_call x1, Pallas kernels, local(): pl.pallas_call(functools.partial(potential_kernel, devices), out_shape=ja...  13.3 us
    unnamed x3, local copies, waits for them, and re-layouts  2.71 us

commit v1 on v0

v1 whole, which is shorter than its diff:
```python
import functools
import math

import jax
import jax.numpy as jnp
from jax import lax
from jax.experimental import pallas as pl
from jax.experimental.pallas import tpu as pltpu
from jax.sharding import PartitionSpec as P

FB = 128
KB = 8
CAP = 4
BLK_DEV = 6
SIDE = 16
LAYER = SIDE * SIDE
CELLS = SIDE * SIDE * SIDE
COLS = 5 * BLK_DEV * FB
ROWS = BLK_DEV * FB
PAIR = 2 * FB
NEAR = 4
BOTH = 6
CHUNK = 4 * LAYER
VMEM_BYTES = 60 * 1024 * 1024

omega = 2.0 / 3.0
four_pi = 4.0 * math.pi
slater = (3.0 / math.pi) ** (1.0 / 3.0)
f32 = jnp.float32
bf16 = jnp.bfloat16


def wrapped(distance):
    moved = distance + 0.5
    return (moved - jnp.floor(moved)) - 0.5


def order_blocks(brick, first, second, bb_ref):
    blocks = [bb_ref[j, brick] for j in range(KB)]
    owners = [block // BLK_DEV for block in blocks]
    keys = [
        jnp.where(owner == first, 0, jnp.where(owner == second, KB, 2 * KB)) + j for j, owner in enumerate(owners)
    ]
    places = [sum((other < key).astype(jnp.int32) for other in keys if other is not key) for key in keys]
    return [
        sum(jnp.where(place == s, block, 0) for place, block in zip(places, blocks)) for s in range(KB)
    ]


def column_block(block, me, devices):
    owner = block // BLK_DEV
    step = jnp.minimum(lax.rem(owner - me + 2 + devices, devices), 4)
    return step * BLK_DEV + lax.rem(block, BLK_DEV)


def pair_of(me):
    return me + 1 - 2 * lax.rem(me, 2)


def across_of(me, devices):
    return lax.rem(me + 2 * lax.rem(me, 2) - 1 + devices, devices)


def factors(block, brick, devices, param_refs):
    point = (lax.broadcasted_iota(jnp.int32, (SIDE, FB), 0).astype(f32) + 0.5) / SIDE
    owner = block // BLK_DEV
    offset = (lax.rem(brick - owner + 1 + devices, devices) - 1).astype(f32)
    mid_x, mid_y, mid_z, rate = [ref[block] for ref in param_refs]
    rate = -rate
    along_x = (offset + point) - mid_x
    along_y = wrapped(point - mid_y)
    along_z = wrapped(point - mid_z)
    return jnp.exp(rate * along_x * along_x), jnp.exp(rate * along_y * along_y), jnp.exp(rate * along_z * along_z)


def plane(factor_y, factor_z, rows_ref):
    for j in range(SIDE):
        rows_ref[j * SIDE : (j + 1) * SIDE, :] = factor_y[j : j + 1] * factor_z
    return rows_ref[...].T


def spread_matrix(spread_ref):
    shape = spread_ref.shape
    source = lax.rem(lax.broadcasted_iota(jnp.int32, shape, 0), SIDE)
    target = lax.broadcasted_iota(jnp.int32, shape, 1) // FB
    spread_ref[...] = jnp.where(source == target, 1.0, 0.0).astype(bf16)


def fill_block(which, a, brick, devices, slot_ref, param_refs, rows_ref, spread_ref, orb_ref):
    factor_x, factor_y, factor_z = factors(slot_ref[which, a], brick, devices, param_refs)
    high = factor_x.astype(bf16)
    rest = factor_x - high.astype(f32)
    middle = rest.astype(bf16)
    low = (rest - middle.astype(f32)).astype(bf16)
    parts = jnp.concatenate([high, middle, low], axis=0)
    factor_yz = plane(factor_y, factor_z, rows_ref)
    start = pl.multiple_of(a * FB, FB)
    for n in range(SIDE // 2):
        wide = lax.dot_general(
            parts,
            spread_ref[:, n * PAIR : (n + 1) * PAIR],
            (((0,), (0,)), ((), ())),
            preferred_element_type=f32,
        )
        for h in range(2):
            one = wide[:, h * FB : (h + 1) * FB]
            i = 2 * n + h
            orb_ref[pl.ds(start, FB), i * LAYER : (i + 1) * LAYER] = jnp.concatenate(
                [one * factor_yz[:, :FB], one * factor_yz[:, FB:]], axis=1
            ).astype(bf16)


def fold(mat_ref, pairs):
    for i in range(pairs):
        for j in range(i + 1, pairs):
            above = mat_ref[i * PAIR : (i + 1) * PAIR, j * PAIR : (j + 1) * PAIR].astype(f32)
            below = mat_ref[j * PAIR : (j + 1) * PAIR, i * PAIR : (i + 1) * PAIR].astype(f32)
            mat_ref[i * PAIR : (i + 1) * PAIR, j * PAIR : (j + 1) * PAIR] = (above + below.T).astype(bf16)


def density_chunk(j, pairs, mat_ref, orb_ref, pd_ref, t):
    cells = pl.ds(pl.multiple_of(j * CHUNK, CHUNK), CHUNK)
    total = jnp.zeros((1, CHUNK), f32)
    for i in range(pairs):
        applied = jnp.dot(
            mat_ref[i * PAIR : (i + 1) * PAIR, i * PAIR :], orb_ref[i * PAIR :, cells], preferred_element_type=f32
        )
        own = orb_ref[i * PAIR : (i + 1) * PAIR, cells].astype(f32)
        total = total + jnp.sum(own * applied, axis=0, keepdims=True)
    for q in range(CHUNK // LAYER):
        pd_ref[t, pl.ds(j * (CHUNK // LAYER) + q, 1), :] = total[:, q * LAYER : (q + 1) * LAYER]


def weigh_block(k, orb_ref, pot_ref, t, wei_ref):
    rows = pl.ds(pl.multiple_of(k * FB, FB), FB)
    for i in range(SIDE):
        cells = slice(i * LAYER, (i + 1) * LAYER)
        level = pot_ref[t, i : i + 1, :] * (64.0 / CELLS)
        wei_ref[rows, cells] = (orb_ref[rows, cells].astype(f32) * level).astype(bf16)


def ham_column(j, pairs, wei_ref, orb_ref, tile_ref):
    rows = PAIR * min(j + 1, pairs)
    here = slice(j * PAIR, (j + 1) * PAIR)
    tile = lax.dot_general(
        wei_ref[0:rows, :], orb_ref[here, :], (((1,), (1,)), ((), ())), preferred_element_type=f32
    )
    tile_ref[0:rows, here] = tile
    if j < pairs:
        for i in range(j):
            tile_ref[here, i * PAIR : (i + 1) * PAIR] = tile[i * PAIR : (i + 1) * PAIR].T


def potential_of(density, before, after, average):
    scale = omega * four_pi / 6.0
    lane = lax.broadcasted_iota(jnp.int32, (SIDE, LAYER), 1) % SIDE
    row = lax.broadcasted_iota(jnp.int32, (SIDE, LAYER), 0)

    def moved(x, steps, axis):
        return pltpu.roll(x, steps % x.shape[axis], axis)

    source = density - average
    one = scale * source
    up = jnp.where(row == 0, scale * (before - average), moved(one, 1, 0))
    down = jnp.where(row == SIDE - 1, scale * (after - average), moved(one, -1, 0))
    beside = up + down + moved(one, SIDE, 1) + moved(one, -SIDE, 1)
    beside = beside + jnp.where(lane == 0, moved(one, 1 - SIDE, 1), moved(one, 1, 1))
    beside = beside + jnp.where(lane == SIDE - 1, moved(one, SIDE - 1, 1), moved(one, -1, 1))
    two = one + omega * ((four_pi * source + beside) / 6.0 - one)
    size = jnp.abs(density)
    safe = jnp.where(size > 0.0, size, 1.0)
    root = jnp.exp(jnp.log(safe) / 3.0)
    root = root - (root - safe / (root * root)) / 3.0
    root = jnp.where(size > 0.0, root, 0.0)
    root = jnp.where(density < 0.0, -root, root)
    return two - slater * root


def main_kernel(
    devices,
    bb_ref,
    rows_hbm,
    cx,
    cy,
    cz,
    ex,
    out_ref,
    tiles_hbm,
    rows_vmem,
    orb_a,
    orb_b,
    mat_a,
    mat_b,
    mat_in,
    mat_out,
    wei_a,
    wei_b,
    tile_a,
    tile_b,
    plane_ref,
    spread_ref,
    pd_ref,
    pot_ref,
    sum_ref,
    full_in,
    before_in,
    after_in,
    sums,
    slot_ref,
    col_ref,
    load_sem,
    mat_sem,
    send_sem,
    recv_sem,
    all_sem,
    tile_sem,
    tile_send,
    tile_recv,
):
    me = lax.axis_index("dev")
    odd = lax.rem(me, 2)
    pair = pair_of(me)
    across = across_of(me, devices)
    barrier = pltpu.get_barrier_semaphore()

    def at(step):
        return lax.rem(me + step + devices, devices)

    def greet(k, carry):
        pl.semaphore_signal(barrier, inc=1, device_id=(at(k),), device_id_type=pl.DeviceIdType.MESH)
        return carry

    def load(c, carry):
        col = pl.ds(pl.multiple_of(c * FB, FB), FB)
        pltpu.make_async_copy(rows_hbm.at[:, :, col], rows_vmem.at[:, c], load_sem).start()
        return carry

    lax.fori_loop(0, 5 * BLK_DEV, load, 0)
    lax.fori_loop(1, devices, greet, 0)

    lists = ((across, me, me), (me, pair, me), (pair, me, pair))
    for which, (brick, first, second) in enumerate(lists):
        for s, block in enumerate(order_blocks(brick, first, second, bb_ref)):
            slot_ref[which, s] = block
            col_ref[which, s] = column_block(block, me, devices)

    params = (cx, cy, cz, ex)
    spread_matrix(spread_ref)

    def fill_a(a, carry):
        fill_block(0, a, across, devices, slot_ref, params, plane_ref, spread_ref, orb_a)
        return carry

    def fill_b(a, carry):
        fill_block(1, a, me, devices, slot_ref, params, plane_ref, spread_ref, orb_b)
        return carry

    lax.fori_loop(0, KB, fill_a, 0)
    pltpu.make_async_copy(rows_vmem, rows_vmem, load_sem).wait()

    def gather(which, a, target, other=None):
        block = slot_ref[which, a]
        mine = (block // BLK_DEV == me).astype(f32)
        mask = jnp.full((FB, FB), mine, f32).astype(bf16)
        row = lax.rem(block, BLK_DEV)
        here = slice(a * FB, (a + 1) * FB)
        for c in range(KB):
            there = slice(c * FB, (c + 1) * FB)
            tile = rows_vmem[row, col_ref[which, c]] * mask
            target[here, there] = tile if other is None else tile + other[here, there]

    for a in range(NEAR):
        gather(2, a, mat_out)
    pl.semaphore_wait(barrier, devices - 1)
    for a in range(NEAR):
        gather(0, a, mat_a)
    give = pltpu.make_async_remote_copy(
        src_ref=mat_out,
        dst_ref=mat_in,
        send_sem=mat_sem.at[0],
        recv_sem=mat_sem.at[1],
        device_id=(pair,),
        device_id_type=pl.DeviceIdType.MESH,
    )
    give.start()
    fold(mat_a, 2)
    lax.fori_loop(0, KB, fill_b, 0)

    def density_a(j, carry):
        density_chunk(j, 2, mat_a, orb_a, pd_ref, odd)
        return carry

    def density_b(j, carry):
        density_chunk(j, 3, mat_b, orb_b, pd_ref, 1 - odd)
        return carry

    lax.fori_loop(0, CELLS // CHUNK, density_a, 0)
    give.wait()
    mat_b[0:PAIR, :] = mat_in[0:PAIR, :]
    for a in range(2, NEAR):
        gather(1, a, mat_b, mat_in)
    for a in range(NEAR, BOTH):
        gather(1, a, mat_b)
    fold(mat_b, 3)
    lax.fori_loop(0, CELLS // CHUNK, density_b, 0)
    layer = jnp.sum(pd_ref[0] + pd_ref[1], axis=0, keepdims=True)
    sum_ref[0] = layer[:, :FB] + layer[:, FB:]

    def to_all(k):
        return pltpu.make_async_remote_copy(
            src_ref=sum_ref.at[0],
            dst_ref=sums.at[k - 1],
            send_sem=all_sem.at[0],
            recv_sem=all_sem.at[1],
            device_id=(at(k),),
            device_id_type=pl.DeviceIdType.MESH,
        )

    def start_sum(k, carry):
        to_all(k).start()
        return carry

    low = lax.rem(me - 1 + odd + devices, devices)
    plan = (
        (pd_ref, full_in, across, 0),
        (pd_ref.at[1, pl.ds(8, 8)], before_in.at[odd], lax.rem(low + 2, devices), 1 + odd),
        (pd_ref.at[1, pl.ds(8, 8)], before_in.at[odd], lax.rem(low + 3, devices), 1 + odd),
        (pd_ref.at[0, pl.ds(0, 8)], after_in.at[odd], lax.rem(low - 2 + devices, devices), 3 + odd),
        (pd_ref.at[0, pl.ds(0, 8)], after_in.at[odd], lax.rem(low - 1 + devices, devices), 3 + odd),
    )
    copies = [
        pltpu.make_async_remote_copy(
            src_ref=src,
            dst_ref=dst,
            send_sem=send_sem.at[q],
            recv_sem=recv_sem.at[r],
            device_id=(device,),
            device_id_type=pl.DeviceIdType.MESH,
        )
        for q, (src, dst, device, r) in enumerate(plan)
    ]
    lax.fori_loop(1, devices, start_sum, 0)
    for copy in copies:
        copy.start()
    pltpu.make_async_copy(full_in, full_in, recv_sem.at[0]).wait()
    for s in range(2):
        pltpu.make_async_copy(before_in.at[s], before_in.at[s], recv_sem.at[1 + s]).wait()
        pltpu.make_async_copy(after_in.at[s], after_in.at[s], recv_sem.at[3 + s]).wait()
    pltpu.make_async_copy(sums, sums, all_sem.at[1]).wait()

    total = jnp.sum(sums[...], axis=0) + sum_ref[0]
    average = jnp.sum(total, axis=1, keepdims=True) / (devices * CELLS)
    first = pd_ref[0] + full_in[0]
    second = pd_ref[1] + full_in[1]
    behind = (before_in[0] + before_in[1])[7:]
    ahead = (after_in[0] + after_in[1])[:1]
    pot_ref[0] = potential_of(first, behind, second[:1], average)
    pot_ref[1] = potential_of(second, first[SIDE - 1 :], ahead, average)
    out_ref[...] = pot_ref[1 - odd]

    def weigh_a(k, carry):
        weigh_block(k, orb_a, pot_ref, odd, wei_a)
        return carry

    def weigh_b(k, carry):
        weigh_block(k, orb_b, pot_ref, 1 - odd, wei_b)
        return carry

    lax.fori_loop(0, BOTH, weigh_b, 0)

    def give_tiles(n, cells):
        return pltpu.make_async_remote_copy(
            src_ref=tile_b.at[pl.ds(0, NEAR * FB), cells],
            dst_ref=tiles_hbm.at[2, :, cells],
            send_sem=tile_send.at[n],
            recv_sem=tile_recv.at[n],
            device_id=(pair,),
            device_id_type=pl.DeviceIdType.MESH,
        )

    gives = [give_tiles(0, pl.ds(0, 2 * PAIR)), give_tiles(1, pl.ds(2 * PAIR, PAIR)), give_tiles(2, pl.ds(3 * PAIR, PAIR))]
    ham_column(0, 3, wei_b, orb_b, tile_b)
    ham_column(1, 3, wei_b, orb_b, tile_b)
    gives[0].start()
    ham_column(2, 3, wei_b, orb_b, tile_b)
    gives[1].start()
    ham_column(3, 3, wei_b, orb_b, tile_b)
    gives[2].start()
    keep_b = pltpu.make_async_copy(tile_b.at[pl.ds(PAIR, NEAR * FB)], tiles_hbm.at[1], tile_sem.at[1])
    keep_b.start()
    lax.fori_loop(0, NEAR, weigh_a, 0)
    for j in range(4):
        ham_column(j, 2, wei_a, orb_a, tile_a)
    keep_a = pltpu.make_async_copy(tile_a, tiles_hbm.at[0], tile_sem.at[0])
    keep_a.start()
    for copy in copies:
        copy.wait_send()
    pltpu.make_async_copy(sums, sums, all_sem.at[0]).wait()
    for copy in gives:
        copy.wait()
    keep_b.wait()
    keep_a.wait()


def out_kernel(devices, bb_ref, pot_in, tiles_hbm, pot_out, ham_hbm, acc_ref, tiles, slot_ref, col_ref, in_sem, out_sem):
    me = lax.axis_index("dev")
    pair = pair_of(me)
    across = across_of(me, devices)
    lists = ((across, me, me), (me, pair, me), (pair, me, pair))
    first_slot = (0, 2, 0)
    for which, (brick, first, second) in enumerate(lists):
        for s, block in enumerate(order_blocks(brick, first, second, bb_ref)):
            slot_ref[which, s] = block
            col_ref[which, s] = column_block(block, me, devices)

    def place(which, r):
        return sum(
            jnp.where(slot_ref[which, first_slot[which] + s] == me * BLK_DEV + r, s + 1, 0) for s in range(CAP)
        )

    def fetch(which, s):
        rows = pl.ds(pl.multiple_of(s * FB, FB), FB)
        return pltpu.make_async_copy(tiles_hbm.at[which, rows], tiles.at[which, rows], in_sem.at[which, s])

    places = [[place(which, r) for which in range(3)] for r in range(BLK_DEV)]
    for r in range(BLK_DEV):
        for which in range(3):

            @pl.when(places[r][which] > 0)
            def _():
                fetch(which, places[r][which] - 1).start()

    for i in range(SIDE):
        pot_out[:, i * LAYER : (i + 1) * LAYER] = pot_in[i : i + 1, :]
    stores = []
    for r in range(BLK_DEV):
        here = slice(r * FB, (r + 1) * FB)
        acc_ref[here, :] = jnp.zeros((FB, COLS), f32)
        for which in range(3):

            @pl.when(places[r][which] > 0)
            def _():
                s = places[r][which] - 1
                fetch(which, s).wait()
                rows = pl.ds(pl.multiple_of(s * FB, FB), FB)
                for c in range(KB):
                    col = pl.ds(pl.multiple_of(col_ref[which, c] * FB, FB), FB)
                    acc_ref[here, col] += tiles[which, rows, c * FB : (c + 1) * FB]

        store = pltpu.make_async_copy(acc_ref.at[here], ham_hbm.at[here], out_sem.at[r])
        store.start()
        stores.append(store)
    for store in stores:
        store.wait()


def local(devices, density_rows, center_x, center_y, center_z, exponent, brick_blocks):
    params = [x.reshape(-1, 1, FB) for x in (center_x, center_y, center_z, exponent)]
    blocks = brick_blocks.T
    vmem = pl.BlockSpec(memory_space=pltpu.VMEM)
    smem = pl.BlockSpec(memory_space=pltpu.SMEM)
    anywhere = pl.BlockSpec(memory_space=pl.ANY)
    potential, tiles = pl.pallas_call(
        functools.partial(main_kernel, devices),
        out_shape=(
            jax.ShapeDtypeStruct((SIDE, LAYER), f32),
            jax.ShapeDtypeStruct((3, NEAR * FB, KB * FB), f32),
        ),
        in_specs=[smem, anywhere] + [vmem] * 4,
        out_specs=(vmem, anywhere),
        scratch_shapes=[
            pltpu.VMEM((BLK_DEV, 5 * BLK_DEV, FB, FB), bf16),
            pltpu.VMEM((KB * FB, CELLS), bf16),
            pltpu.VMEM((KB * FB, CELLS), bf16),
            pltpu.VMEM((NEAR * FB, KB * FB), bf16),
            pltpu.VMEM((BOTH * FB, KB * FB), bf16),
            pltpu.VMEM((NEAR * FB, KB * FB), bf16),
            pltpu.VMEM((NEAR * FB, KB * FB), bf16),
            pltpu.VMEM((NEAR * FB, CELLS), bf16),
            pltpu.VMEM((BOTH * FB, CELLS), bf16),
            pltpu.VMEM((NEAR * FB, KB * FB), f32),
            pltpu.VMEM((BOTH * FB, KB * FB), f32),
            pltpu.VMEM((LAYER, FB), f32),
            pltpu.VMEM((3 * SIDE, SIDE * FB), bf16),
            pltpu.VMEM((2, SIDE, LAYER), f32),
            pltpu.VMEM((2, SIDE, LAYER), f32),
            pltpu.VMEM((1, 1, FB), f32),
            pltpu.VMEM((2, SIDE, LAYER), f32),
            pltpu.VMEM((2, 8, LAYER), f32),
            pltpu.VMEM((2, 8, LAYER), f32),
            pltpu.VMEM((devices - 1, 1, FB), f32),
            pltpu.SMEM((3, KB), jnp.int32),
            pltpu.SMEM((3, KB), jnp.int32),
            pltpu.SemaphoreType.DMA,
            pltpu.SemaphoreType.DMA((2,)),
            pltpu.SemaphoreType.DMA((5,)),
            pltpu.SemaphoreType.DMA((5,)),
            pltpu.SemaphoreType.DMA((2,)),
            pltpu.SemaphoreType.DMA((2,)),
            pltpu.SemaphoreType.DMA((3,)),
            pltpu.SemaphoreType.DMA((3,)),
        ],
        compiler_params=pltpu.CompilerParams(collective_id=0, has_side_effects=True, vmem_limit_bytes=VMEM_BYTES),
        name="build_tiles",
    )(blocks, density_rows.reshape(BLK_DEV, FB, COLS), *params)
    return pl.pallas_call(
        functools.partial(out_kernel, devices),
        out_shape=(jax.ShapeDtypeStruct((1, CELLS), f32), jax.ShapeDtypeStruct((ROWS, COLS), f32)),
        in_specs=[smem, vmem, anywhere],
        out_specs=(vmem, anywhere),
        scratch_shapes=[
            pltpu.VMEM((ROWS, COLS), f32),
            pltpu.VMEM((3, NEAR * FB, KB * FB), f32),
            pltpu.SMEM((3, KB), jnp.int32),
            pltpu.SMEM((3, KB), jnp.int32),
            pltpu.SemaphoreType.DMA((3, CAP)),
            pltpu.SemaphoreType.DMA((BLK_DEV,)),
        ],
        compiler_params=pltpu.CompilerParams(vmem_limit_bytes=VMEM_BYTES),
        name="place_tiles",
    )(blocks, potential, tiles)


def solution(mesh):
    placed = (P("dev", None), P(), P(), P(), P(), P())
    return jax.shard_map(
        functools.partial(local, mesh.shape["dev"]),
        mesh=mesh,
        in_specs=placed,
        out_specs=(P("dev", None), P("dev", None)),
        check_vma=False,
    )
```

time: 78.4 us -> 55.6 us (0.71)
  Pallas kernels: 74.6 us -> 54.6 us
  local copies, waits for them, and re-layouts: 2.71 us -> 0 us
    pallas_call x3 -> x2, Pallas kernels: 74.6 us -> 54.6 us  [the longest x1 46.7 us: local(): pl.pallas_call(functools.partial(main_kernel, devices), out_shape=(jax.Sh...]
    unnamed x3 -> x0, local copies, waits for them, and re-layouts: 2.71 us -> none
where the time goes in v1:
time: 55.6 us; the launch traced here: 55.4 us
  Pallas kernels  54.6 us (98%)
  between operations  0.8 us (1%)
    pallas_call x1, Pallas kernels, local(): pl.pallas_call(functools.partial(main_kernel, devices), out_shape=(jax.Sh...  46.7 us
    pallas_call x1, Pallas kernels, local(): pl.pallas_call(functools.partial(out_kernel, devices), out_shape=(jax.Sha...  7.87 us

profile of v1, /device:TPU:0, one launch (start us, length us, event | category | flops | bytes accessed | tf_op | source)
XLA Modules:
  0.0 55.4 jit_solution(6729047260975492744)
XLA Ops:
  0.6 46.7 %build_tiles.1 = (f32[16,256]{1,0:T(8,128)}, f32[3,512,1024]{2,1,0:T(8,128)}) custom-call(s32[8,32]{1,0:T(8,128)} %bitcast.11, bf16[6,128,3840]{2,1,0:T(8,128)(2,1)} %bitcast.6, f32[192,1,128]{2,1,0:T(1,128)} %bitcast.7, f32[192,1,128]{2,1,0:T(1,128)} %bitcast.8, f32[192,1,128]{2,1,0:T(1,128)} %bitcast.9, f32[192,1,128]{2,1,0:T(1,128)} %bitcast.10), custom_call_target="tpu_custom_call" | custom-call | tf_op jit(solution)/shard_map/build_tiles/pallas_call | solution.py:463
  47.3 7.9 %place_tiles.1 = (f32[1,4096]{1,0:T(1,128)}, f32[768,3840]{1,0:T(8,128)}) custom-call(s32[8,32]{1,0:T(8,128)} %bitcast.12, f32[16,256]{1,0:T(8,128)} %get-tuple-element.4.pot_in, f32[3,512,1024]{2,1,0:T(8,128)} %get-tuple-element.5.tiles_hbm), custom_call_target="tpu_custom_call" | custom-call | tf_op jit(solution)/shard_map/place_tiles/pallas_call | solution.py:506

commit v2 on v1

--- a/solution.py
+++ b/solution.py
@@ -21,7 +21,7 @@
 NEAR = 4
 BOTH = 6
 CHUNK = 4 * LAYER
-VMEM_BYTES = 60 * 1024 * 1024
+VMEM_BYTES = 46 * 1024 * 1024
 
 omega = 2.0 / 3.0
 four_pi = 4.0 * math.pi
@@ -35,22 +35,34 @@
     return (moved - jnp.floor(moved)) - 0.5
 
 
-def order_blocks(brick, first, second, bb_ref):
-    blocks = [bb_ref[j, brick] for j in range(KB)]
-    owners = [block // BLK_DEV for block in blocks]
-    keys = [
-        jnp.where(owner == first, 0, jnp.where(owner == second, KB, 2 * KB)) + j for j, owner in enumerate(owners)
-    ]
-    places = [sum((other < key).astype(jnp.int32) for other in keys if other is not key) for key in keys]
-    return [
-        sum(jnp.where(place == s, block, 0) for place, block in zip(places, blocks)) for s in range(KB)
-    ]
-
-
-def column_block(block, me, devices):
-    owner = block // BLK_DEV
-    step = jnp.minimum(lax.rem(owner - me + 2 + devices, devices), 4)
-    return step * BLK_DEV + lax.rem(block, BLK_DEV)
+SORT = (
+    ((0, 1), (2, 3), (4, 5), (6, 7)),
+    ((0, 2), (1, 3), (4, 6), (5, 7)),
+    ((1, 2), (5, 6)),
+    ((0, 4), (1, 5), (2, 6), (3, 7)),
+    ((2, 4), (3, 5)),
+    ((1, 2), (3, 4), (5, 6)),
+)
+
+
+def order_blocks(which, brick, first, second, me, devices, bb_ref, slot_ref, col_ref):
+    keys = []
+    for j in range(KB):
+        block = bb_ref[j, brick]
+        owner = lax.div(block, BLK_DEV)
+        rank = jnp.where(owner == first, 0, jnp.where(owner == second, 1 << 20, 2 << 20))
+        keys.append(rank + (owner * 8 + (block - owner * BLK_DEV)))
+    for layer in SORT:
+        for i, j in layer:
+            keys[i], keys[j] = jnp.minimum(keys[i], keys[j]), jnp.maximum(keys[i], keys[j])
+    for s, key in enumerate(keys):
+        code = key & ((1 << 20) - 1)
+        owner = code >> 3
+        local = code & 7
+        step = owner - me + 2
+        step = jnp.where(step < 0, step + devices, jnp.where(step >= devices, step - devices, step))
+        slot_ref[which, s] = owner * BLK_DEV + local
+        col_ref[which, s] = jnp.minimum(step, 4) * BLK_DEV + local
 
 
 def pair_of(me):
@@ -63,7 +75,7 @@
 
 def factors(block, brick, devices, param_refs):
     point = (lax.broadcasted_iota(jnp.int32, (SIDE, FB), 0).astype(f32) + 0.5) / SIDE
-    owner = block // BLK_DEV
+    owner = lax.div(block, BLK_DEV)
     offset = (lax.rem(brick - owner + 1 + devices, devices) - 1).astype(f32)
     mid_x, mid_y, mid_z, rate = [ref[block] for ref in param_refs]
     rate = -rate
@@ -110,6 +122,15 @@
             ).astype(bf16)
 
 
+def fill_lanes(which, a, brick, devices, slot_ref, param_refs, rows_ref, orb_ref):
+    factor_x, factor_y, factor_z = factors(slot_ref[which, a], brick, devices, param_refs)
+    along = factor_x.T
+    factor_yz = plane(factor_y, factor_z, rows_ref)
+    start = pl.multiple_of(a * FB, FB)
+    for i in range(SIDE):
+        orb_ref[pl.ds(start, FB), i * LAYER : (i + 1) * LAYER] = (along[:, i : i + 1] * factor_yz).astype(bf16)
+
+
 def fold(mat_ref, pairs):
     for i in range(pairs):
         for j in range(i + 1, pairs):
@@ -139,13 +160,16 @@
         wei_ref[rows, cells] = (orb_ref[rows, cells].astype(f32) * level).astype(bf16)
 
 
+def ham_tile(rows, j, wei_ref, orb_ref):
+    here = slice(j * PAIR, (j + 1) * PAIR)
+    return lax.dot_general(wei_ref[rows, :], orb_ref[here, :], (((1,), (1,)), ((), ())), preferred_element_type=f32)
+
+
 def ham_column(j, pairs, wei_ref, orb_ref, tile_ref):
-    rows = PAIR * min(j + 1, pairs)
+    rows = slice(0, PAIR * min(j + 1, pairs))
     here = slice(j * PAIR, (j + 1) * PAIR)
-    tile = lax.dot_general(
-        wei_ref[0:rows, :], orb_ref[here, :], (((1,), (1,)), ((), ())), preferred_element_type=f32
-    )
-    tile_ref[0:rows, here] = tile
+    tile = ham_tile(rows, j, wei_ref, orb_ref)
+    tile_ref[rows, here] = tile
     if j < pairs:
         for i in range(j):
             tile_ref[here, i * PAIR : (i + 1) * PAIR] = tile[i * PAIR : (i + 1) * PAIR].T
@@ -185,18 +209,17 @@
     cz,
     ex,
     out_ref,
+    orb_a,
+    wei_a,
+    tile_b,
     tiles_hbm,
     rows_vmem,
-    orb_a,
     orb_b,
     mat_a,
     mat_b,
     mat_in,
     mat_out,
-    wei_a,
     wei_b,
-    tile_a,
-    tile_b,
     plane_ref,
     spread_ref,
     pd_ref,
@@ -213,7 +236,6 @@
     send_sem,
     recv_sem,
     all_sem,
-    tile_sem,
     tile_send,
     tile_recv,
 ):
@@ -240,33 +262,29 @@
 
     lists = ((across, me, me), (me, pair, me), (pair, me, pair))
     for which, (brick, first, second) in enumerate(lists):
-        for s, block in enumerate(order_blocks(brick, first, second, bb_ref)):
-            slot_ref[which, s] = block
-            col_ref[which, s] = column_block(block, me, devices)
+        order_blocks(which, brick, first, second, me, devices, bb_ref, slot_ref, col_ref)
 
     params = (cx, cy, cz, ex)
     spread_matrix(spread_ref)
 
     def fill_a(a, carry):
-        fill_block(0, a, across, devices, slot_ref, params, plane_ref, spread_ref, orb_a)
-        return carry
-
-    def fill_b(a, carry):
-        fill_block(1, a, me, devices, slot_ref, params, plane_ref, spread_ref, orb_b)
-        return carry
-
-    lax.fori_loop(0, KB, fill_a, 0)
+        for h in range(2):
+            fill_block(0, 2 * a + h, across, devices, slot_ref, params, plane_ref.at[h], spread_ref, orb_a)
+        return carry
+
+    lax.fori_loop(0, KB // 2, fill_a, 0)
     pltpu.make_async_copy(rows_vmem, rows_vmem, load_sem).wait()
 
     def gather(which, a, target, other=None):
         block = slot_ref[which, a]
-        mine = (block // BLK_DEV == me).astype(f32)
-        mask = jnp.full((FB, FB), mine, f32).astype(bf16)
-        row = lax.rem(block, BLK_DEV)
+        owner = lax.div(block, BLK_DEV)
+        mask = jnp.full((FB, PAIR), (owner == me).astype(f32), f32).astype(bf16)
+        row = block - owner * BLK_DEV
         here = slice(a * FB, (a + 1) * FB)
-        for c in range(KB):
-            there = slice(c * FB, (c + 1) * FB)
-            tile = rows_vmem[row, col_ref[which, c]] * mask
+        for c in range(0, KB, 2):
+            there = slice(c * FB, (c + 2) * FB)
+            tiles = [rows_vmem[row, col_ref[which, c + h]] for h in range(2)]
+            tile = jnp.concatenate(tiles, axis=1) * mask
             target[here, there] = tile if other is None else tile + other[here, there]
 
     for a in range(NEAR):
@@ -284,9 +302,10 @@
     )
     give.start()
     fold(mat_a, 2)
-    lax.fori_loop(0, KB, fill_b, 0)
 
     def density_a(j, carry):
+        for h in range(2):
+            fill_lanes(1, 2 * j + h, me, devices, slot_ref, params, plane_ref.at[h], orb_b)
         density_chunk(j, 2, mat_a, orb_a, pd_ref, odd)
         return carry
 
@@ -371,87 +390,122 @@
     def give_tiles(n, cells):
         return pltpu.make_async_remote_copy(
             src_ref=tile_b.at[pl.ds(0, NEAR * FB), cells],
-            dst_ref=tiles_hbm.at[2, :, cells],
+            dst_ref=tiles_hbm.at[:, cells],
             send_sem=tile_send.at[n],
             recv_sem=tile_recv.at[n],
             device_id=(pair,),
             device_id_type=pl.DeviceIdType.MESH,
         )
 
-    gives = [give_tiles(0, pl.ds(0, 2 * PAIR)), give_tiles(1, pl.ds(2 * PAIR, PAIR)), give_tiles(2, pl.ds(3 * PAIR, PAIR))]
-    ham_column(0, 3, wei_b, orb_b, tile_b)
-    ham_column(1, 3, wei_b, orb_b, tile_b)
+    gives = [give_tiles(n, pl.ds(n * PAIR, PAIR)) for n in range(4)]
+    for j in (3, 2):
+        ham_column(j, 2, wei_b, orb_b, tile_b)
+        weigh_a(3 - j, 0)
+        gives[j].start()
+    ham_column(1, 2, wei_b, orb_b, tile_b)
+    weigh_a(2, 0)
+    gives[1].start()
+    ham_column(0, 2, wei_b, orb_b, tile_b)
     gives[0].start()
-    ham_column(2, 3, wei_b, orb_b, tile_b)
-    gives[1].start()
-    ham_column(3, 3, wei_b, orb_b, tile_b)
-    gives[2].start()
-    keep_b = pltpu.make_async_copy(tile_b.at[pl.ds(PAIR, NEAR * FB)], tiles_hbm.at[1], tile_sem.at[1])
-    keep_b.start()
-    lax.fori_loop(0, NEAR, weigh_a, 0)
-    for j in range(4):
-        ham_column(j, 2, wei_a, orb_a, tile_a)
-    keep_a = pltpu.make_async_copy(tile_a, tiles_hbm.at[0], tile_sem.at[0])
-    keep_a.start()
+    weigh_a(3, 0)
+    for j in (2, 3):
+        tile = ham_tile(slice(2 * PAIR, 3 * PAIR), j, wei_b, orb_b)
+        tile_b[2 * PAIR : 3 * PAIR, j * PAIR : (j + 1) * PAIR] = tile
+    for i in range(2):
+        tile_b[2 * PAIR : 3 * PAIR, i * PAIR : (i + 1) * PAIR] = tile_b[
+            i * PAIR : (i + 1) * PAIR, 2 * PAIR : 3 * PAIR
+        ].T
     for copy in copies:
         copy.wait_send()
     pltpu.make_async_copy(sums, sums, all_sem.at[0]).wait()
     for copy in gives:
         copy.wait()
-    keep_b.wait()
-    keep_a.wait()
-
-
-def out_kernel(devices, bb_ref, pot_in, tiles_hbm, pot_out, ham_hbm, acc_ref, tiles, slot_ref, col_ref, in_sem, out_sem):
+
+
+def out_kernel(
+    devices,
+    bb_ref,
+    pot_in,
+    orb_a,
+    wei_a,
+    tile_b,
+    tiles_hbm,
+    pot_out,
+    ham_hbm,
+    acc_ref,
+    tile_a,
+    tile_in,
+    slot_ref,
+    col_ref,
+    in_sem,
+    early_sem,
+    late_sem,
+):
     me = lax.axis_index("dev")
     pair = pair_of(me)
     across = across_of(me, devices)
+    fetch = pltpu.make_async_copy(tiles_hbm, tile_in, in_sem)
+    fetch.start()
     lists = ((across, me, me), (me, pair, me), (pair, me, pair))
+    for which, (brick, first, second) in enumerate(lists):
+        order_blocks(which, brick, first, second, me, devices, bb_ref, slot_ref, col_ref)
+    sources = (tile_a, tile_b, tile_in)
     first_slot = (0, 2, 0)
-    for which, (brick, first, second) in enumerate(lists):
-        for s, block in enumerate(order_blocks(brick, first, second, bb_ref)):
-            slot_ref[which, s] = block
-            col_ref[which, s] = column_block(block, me, devices)
-
-    def place(which, r):
-        return sum(
-            jnp.where(slot_ref[which, first_slot[which] + s] == me * BLK_DEV + r, s + 1, 0) for s in range(CAP)
-        )
-
-    def fetch(which, s):
-        rows = pl.ds(pl.multiple_of(s * FB, FB), FB)
-        return pltpu.make_async_copy(tiles_hbm.at[which, rows], tiles.at[which, rows], in_sem.at[which, s])
-
-    places = [[place(which, r) for which in range(3)] for r in range(BLK_DEV)]
-    for r in range(BLK_DEV):
-        for which in range(3):
-
-            @pl.when(places[r][which] > 0)
-            def _():
-                fetch(which, places[r][which] - 1).start()
+
+    def owned(which, s):
+        block = slot_ref[which, first_slot[which] + s]
+        owner = lax.div(block, BLK_DEV)
+        return owner == me, block - owner * BLK_DEV
+
+    def tile_of(ref, row, which, c):
+        col = pl.multiple_of(col_ref[which, c] * FB, FB)
+        return ref.at[pl.ds(pl.multiple_of(row * FB, FB), FB), pl.ds(col, FB)]
+
+    def add(which):
+        for s in range(CAP):
+            mine, row = owned(which, s)
+            row = jnp.where(mine, row, BLK_DEV)
+            start = (first_slot[which] + s) * FB
+            for c in range(KB):
+                tile_of(acc_ref, row, which, c)[...] += sources[which][start : start + FB, c * FB : (c + 1) * FB]
+
+    odd = lax.rem(me, 2)
+    across_rows = [
+        sum((slot_ref[0, s] == me * BLK_DEV + r).astype(jnp.int32) for s in range(CAP)) > 0 for r in range(BLK_DEV)
+    ]
+    free = pl.ds(pl.multiple_of((1 - odd) * 3 * ROWS, FB), 2 * ROWS)
+    shared = pl.ds(pl.multiple_of(odd * 2 * ROWS, FB), 3 * ROWS)
+
+    def store(r, cols, sem):
+        here = pl.ds(r * FB, FB)
+        return pltpu.make_async_copy(acc_ref.at[here, cols], ham_hbm.at[here, cols], sem.at[r])
 
     for i in range(SIDE):
         pot_out[:, i * LAYER : (i + 1) * LAYER] = pot_in[i : i + 1, :]
-    stores = []
+    acc_ref[...] = jnp.zeros(acc_ref.shape, f32)
+    add(1)
+    fetch.wait()
+    add(2)
+    ham_column(0, 2, wei_a, orb_a, tile_a)
     for r in range(BLK_DEV):
-        here = slice(r * FB, (r + 1) * FB)
-        acc_ref[here, :] = jnp.zeros((FB, COLS), f32)
-        for which in range(3):
-
-            @pl.when(places[r][which] > 0)
-            def _():
-                s = places[r][which] - 1
-                fetch(which, s).wait()
-                rows = pl.ds(pl.multiple_of(s * FB, FB), FB)
-                for c in range(KB):
-                    col = pl.ds(pl.multiple_of(col_ref[which, c] * FB, FB), FB)
-                    acc_ref[here, col] += tiles[which, rows, c * FB : (c + 1) * FB]
-
-        store = pltpu.make_async_copy(acc_ref.at[here], ham_hbm.at[here], out_sem.at[r])
-        store.start()
-        stores.append(store)
-    for store in stores:
-        store.wait()
+        store(r, free, early_sem).start()
+
+        @pl.when(jnp.logical_not(across_rows[r]))
+        def _():
+            store(r, shared, late_sem).start()
+
+    for j in range(1, 4):
+        ham_column(j, 2, wei_a, orb_a, tile_a)
+    add(0)
+    for r in range(BLK_DEV):
+
+        @pl.when(across_rows[r])
+        def _():
+            store(r, shared, late_sem).start()
+
+    for r in range(BLK_DEV):
+        store(r, free, early_sem).wait()
+        store(r, shared, late_sem).wait()
 
 
 def local(devices, density_rows, center_x, center_y, center_z, exponent, brick_blocks):
@@ -460,27 +514,26 @@
     vmem = pl.BlockSpec(memory_space=pltpu.VMEM)
     smem = pl.BlockSpec(memory_space=pltpu.SMEM)
     anywhere = pl.BlockSpec(memory_space=pl.ANY)
-    potential, tiles = pl.pallas_call(
+    potential, orbitals, weighted, tiles, tiles_in = pl.pallas_call(
         functools.partial(main_kernel, devices),
         out_shape=(
             jax.ShapeDtypeStruct((SIDE, LAYER), f32),
-            jax.ShapeDtypeStruct((3, NEAR * FB, KB * FB), f32),
+            pltpu.VMEM((KB * FB, CELLS), bf16),
+            pltpu.VMEM((NEAR * FB, CELLS), bf16),
+            pltpu.VMEM((BOTH * FB, KB * FB), f32),
+            jax.ShapeDtypeStruct((NEAR * FB, KB * FB), f32),
         ),
         in_specs=[smem, anywhere] + [vmem] * 4,
-        out_specs=(vmem, anywhere),
+        out_specs=(vmem, vmem, vmem, vmem, anywhere),
         scratch_shapes=[
             pltpu.VMEM((BLK_DEV, 5 * BLK_DEV, FB, FB), bf16),
-            pltpu.VMEM((KB * FB, CELLS), bf16),
             pltpu.VMEM((KB * FB, CELLS), bf16),
             pltpu.VMEM((NEAR * FB, KB * FB), bf16),
             pltpu.VMEM((BOTH * FB, KB * FB), bf16),
             pltpu.VMEM((NEAR * FB, KB * FB), bf16),
             pltpu.VMEM((NEAR * FB, KB * FB), bf16),
-            pltpu.VMEM((NEAR * FB, CELLS), bf16),
             pltpu.VMEM((BOTH * FB, CELLS), bf16),
-            pltpu.VMEM((NEAR * FB, KB * FB), f32),
-            pltpu.VMEM((BOTH * FB, KB * FB), f32),
-            pltpu.VMEM((LAYER, FB), f32),
+            pltpu.VMEM((2, LAYER, FB), f32),
             pltpu.VMEM((3 * SIDE, SIDE * FB), bf16),
             pltpu.VMEM((2, SIDE, LAYER), f32),
             pltpu.VMEM((2, SIDE, LAYER), f32),
@@ -496,29 +549,31 @@
             pltpu.SemaphoreType.DMA((5,)),
             pltpu.SemaphoreType.DMA((5,)),
             pltpu.SemaphoreType.DMA((2,)),
-            pltpu.SemaphoreType.DMA((2,)),
-            pltpu.SemaphoreType.DMA((3,)),
-            pltpu.SemaphoreType.DMA((3,)),
+            pltpu.SemaphoreType.DMA((4,)),
+            pltpu.SemaphoreType.DMA((4,)),
         ],
         compiler_params=pltpu.CompilerParams(collective_id=0, has_side_effects=True, vmem_limit_bytes=VMEM_BYTES),
         name="build_tiles",
     )(blocks, density_rows.reshape(BLK_DEV, FB, COLS), *params)
+    held = [pltpu.with_memory_space_constraint(x, pltpu.VMEM) for x in (orbitals, weighted, tiles)]
     return pl.pallas_call(
         functools.partial(out_kernel, devices),
         out_shape=(jax.ShapeDtypeStruct((1, CELLS), f32), jax.ShapeDtypeStruct((ROWS, COLS), f32)),
-        in_specs=[smem, vmem, anywhere],
+        in_specs=[smem] + [vmem] * 4 + [anywhere],
         out_specs=(vmem, anywhere),
         scratch_shapes=[
-            pltpu.VMEM((ROWS, COLS), f32),
-            pltpu.VMEM((3, NEAR * FB, KB * FB), f32),
+            pltpu.VMEM((ROWS + FB, COLS), f32),
+            pltpu.VMEM((NEAR * FB, KB * FB), f32),
+            pltpu.VMEM((NEAR * FB, KB * FB), f32),
             pltpu.SMEM((3, KB), jnp.int32),
             pltpu.SMEM((3, KB), jnp.int32),
-            pltpu.SemaphoreType.DMA((3, CAP)),
+            pltpu.SemaphoreType.DMA,
+            pltpu.SemaphoreType.DMA((BLK_DEV,)),
             pltpu.SemaphoreType.DMA((BLK_DEV,)),
         ],
         compiler_params=pltpu.CompilerParams(vmem_limit_bytes=VMEM_BYTES),
         name="place_tiles",
-    )(blocks, potential, tiles)
+    )(blocks, potential, *held, tiles_in)
 
 
 def solution(mesh):

time: 55.6 us -> 46.8 us (0.84)
  Pallas kernels: 54.6 us -> 45.8 us
    pallas_call x1, Pallas kernels: 46.7 us -> 37 us  [local(): pl.pallas_call(functools.partial(main_kernel, devices), out_shape=(jax.Sh...]
    pallas_call x1, Pallas kernels: 7.87 us -> 8.77 us  [local(): pl.pallas_call(functools.partial(out_kernel, devices), out_shape=(jax.Sha...]
where the time goes in v2:
time: 46.8 us; the launch traced here: 46.6 us
  Pallas kernels  45.8 us (98%)
  between operations  0.8 us (2%)
    pallas_call x1, Pallas kernels, local(): pl.pallas_call(functools.partial(main_kernel, devices), out_shape=(jax.Sh...  37 us
    pallas_call x1, Pallas kernels, local(): pl.pallas_call(functools.partial(out_kernel, devices), out_shape=(jax.Sha...  8.77 us

profile of v2, /device:TPU:0, one launch (start us, length us, event | category | flops | bytes accessed | tf_op | source)
XLA Modules:
  0.0 46.6 jit_solution(9788817757434346923)
XLA Ops:
  0.6 37.0 %build_tiles.1 = (f32[16,256]{1,0:T(8,128)}, bf16[1024,4096]{1,0:T(8,128)(2,1)S(1)}, bf16[512,4096]{1,0:T(8,128)(2,1)S(1)}, f32[768,1024]{1,0:T(8,128)S(1)}, f32[512,1024]{1,0:T(8,128)}) custom-call(s32[8,32]{1,0:T(8,128)} %bitcast.11, bf16[6,128,3840]{2,1,0:T(8,128)(2,1)} %bitcast.6, f32[192,1,128]{2,1,0:T(1,128)} %bitcast.7, f32[192,1,128]{2,1,0:T(1,128)} %bitcast.8, ...), custom_call_target="tpu_custom_call" | custom-call | tf_op jit(solution)/shard_map/build_tiles/pallas_call | solution.py:517
  37.6 8.8 %place_tiles.1 = (f32[1,4096]{1,0:T(1,128)}, f32[768,3840]{1,0:T(8,128)}) custom-call(s32[8,32]{1,0:T(8,128)} %bitcast.12, f32[16,256]{1,0:T(8,128)} %get-tuple-element.7.pot_in, bf16[1024,4096]{1,0:T(8,128)(2,1)S(1)} %get-tuple-element.8.orb_a, bf16[512,4096]{1,0:T(8,128)(2,1)S(1)} %get-tuple-element.9.wei_a, f32[768,1024]{1,0:T(8,128)S(1)} %get-tuple-element.10.tile_b, ...), custom_call_target="tpu_custom_call" | custom-call | tf_op jit(solution)/shard_map/place_tiles/pallas_call | solution.py:559

commit v3 on v2

--- a/solution.py
+++ b/solution.py
@@ -21,7 +21,7 @@
 NEAR = 4
 BOTH = 6
 CHUNK = 4 * LAYER
-VMEM_BYTES = 46 * 1024 * 1024
+VMEM_BYTES = 33 * 1024 * 1024
 
 omega = 2.0 / 3.0
 four_pi = 4.0 * math.pi
@@ -212,6 +212,8 @@
     orb_a,
     wei_a,
     tile_b,
+    corner,
+    acc_ref,
     tiles_hbm,
     rows_vmem,
     orb_b,
@@ -289,7 +291,6 @@
 
     for a in range(NEAR):
         gather(2, a, mat_out)
-    pl.semaphore_wait(barrier, devices - 1)
     for a in range(NEAR):
         gather(0, a, mat_a)
     give = pltpu.make_async_remote_copy(
@@ -300,7 +301,6 @@
         device_id=(pair,),
         device_id_type=pl.DeviceIdType.MESH,
     )
-    give.start()
     fold(mat_a, 2)
 
     def density_a(j, carry):
@@ -313,7 +313,10 @@
         density_chunk(j, 3, mat_b, orb_b, pd_ref, 1 - odd)
         return carry
 
-    lax.fori_loop(0, CELLS // CHUNK, density_a, 0)
+    lax.fori_loop(0, 1, density_a, 0)
+    pl.semaphore_wait(barrier, devices - 1)
+    give.start()
+    lax.fori_loop(1, CELLS // CHUNK, density_a, 0)
     give.wait()
     mat_b[0:PAIR, :] = mat_in[0:PAIR, :]
     for a in range(2, NEAR):
@@ -361,6 +364,7 @@
     lax.fori_loop(1, devices, start_sum, 0)
     for copy in copies:
         copy.start()
+    acc_ref[...] = jnp.zeros(acc_ref.shape, f32)
     pltpu.make_async_copy(full_in, full_in, recv_sem.at[0]).wait()
     for s in range(2):
         pltpu.make_async_copy(before_in.at[s], before_in.at[s], recv_sem.at[1 + s]).wait()
@@ -397,24 +401,21 @@
             device_id_type=pl.DeviceIdType.MESH,
         )
 
-    gives = [give_tiles(n, pl.ds(n * PAIR, PAIR)) for n in range(4)]
+    gives = [give_tiles(n, pl.ds(n * 2 * PAIR, 2 * PAIR)) for n in range(2)]
     for j in (3, 2):
         ham_column(j, 2, wei_b, orb_b, tile_b)
         weigh_a(3 - j, 0)
-        gives[j].start()
-    ham_column(1, 2, wei_b, orb_b, tile_b)
-    weigh_a(2, 0)
     gives[1].start()
-    ham_column(0, 2, wei_b, orb_b, tile_b)
+    for j in (1, 0):
+        ham_column(j, 2, wei_b, orb_b, tile_b)
+        weigh_a(3 - j, 0)
     gives[0].start()
-    weigh_a(3, 0)
+    last = slice(2 * PAIR, 3 * PAIR)
     for j in (2, 3):
-        tile = ham_tile(slice(2 * PAIR, 3 * PAIR), j, wei_b, orb_b)
-        tile_b[2 * PAIR : 3 * PAIR, j * PAIR : (j + 1) * PAIR] = tile
+        tile_b[last, j * PAIR : (j + 1) * PAIR] = ham_tile(last, j, wei_b, orb_b)
     for i in range(2):
-        tile_b[2 * PAIR : 3 * PAIR, i * PAIR : (i + 1) * PAIR] = tile_b[
-            i * PAIR : (i + 1) * PAIR, 2 * PAIR : 3 * PAIR
-        ].T
+        tile_b[last, i * PAIR : (i + 1) * PAIR] = tile_b[i * PAIR : (i + 1) * PAIR, last].T
+    corner[...] = ham_tile(slice(0, PAIR), 0, wei_a, orb_a)
     for copy in copies:
         copy.wait_send()
     pltpu.make_async_copy(sums, sums, all_sem.at[0]).wait()
@@ -424,28 +425,38 @@
 
 def out_kernel(
     devices,
-    bb_ref,
+    bb_hbm,
     pot_in,
     orb_a,
     wei_a,
     tile_b,
+    corner,
+    acc_in,
     tiles_hbm,
     pot_out,
     ham_hbm,
     acc_ref,
     tile_a,
     tile_in,
+    bb_ref,
     slot_ref,
     col_ref,
     in_sem,
+    bb_sem,
     early_sem,
     late_sem,
 ):
     me = lax.axis_index("dev")
     pair = pair_of(me)
     across = across_of(me, devices)
+    lay = pltpu.make_async_copy(bb_hbm, bb_ref, bb_sem)
+    lay.start()
     fetch = pltpu.make_async_copy(tiles_hbm, tile_in, in_sem)
     fetch.start()
+    for i in range(SIDE):
+        pot_out[:, i * LAYER : (i + 1) * LAYER] = pot_in[i : i + 1, :]
+    tile_a[0:PAIR, 0:PAIR] = corner[...]
+    lay.wait()
     lists = ((across, me, me), (me, pair, me), (pair, me, pair))
     for which, (brick, first, second) in enumerate(lists):
         order_blocks(which, brick, first, second, me, devices, bb_ref, slot_ref, col_ref)
@@ -469,10 +480,25 @@
             for c in range(KB):
                 tile_of(acc_ref, row, which, c)[...] += sources[which][start : start + FB, c * FB : (c + 1) * FB]
 
-    odd = lax.rem(me, 2)
     across_rows = [
         sum((slot_ref[0, s] == me * BLK_DEV + r).astype(jnp.int32) for s in range(CAP)) > 0 for r in range(BLK_DEV)
     ]
+
+    def store_row(r):
+        here = pl.ds(r * FB, FB)
+        return pltpu.make_async_copy(acc_ref.at[here], ham_hbm.at[here], early_sem.at[r])
+
+    def each_tile(act):
+        for s in range(CAP):
+            mine, row = owned(0, s)
+
+            @pl.when(mine)
+            def _():
+                for c in range(KB):
+                    source, target = tile_of(acc_ref, row, 0, c), tile_of(ham_hbm, row, 0, c)
+                    act(pltpu.make_async_copy(source, target, late_sem.at[s, c]))
+
+    odd = lax.rem(me, 2)
     free = pl.ds(pl.multiple_of((1 - odd) * 3 * ROWS, FB), 2 * ROWS)
     shared = pl.ds(pl.multiple_of(odd * 2 * ROWS, FB), 3 * ROWS)
 
@@ -480,13 +506,9 @@
         here = pl.ds(r * FB, FB)
         return pltpu.make_async_copy(acc_ref.at[here, cols], ham_hbm.at[here, cols], sem.at[r])
 
-    for i in range(SIDE):
-        pot_out[:, i * LAYER : (i + 1) * LAYER] = pot_in[i : i + 1, :]
-    acc_ref[...] = jnp.zeros(acc_ref.shape, f32)
     add(1)
     fetch.wait()
     add(2)
-    ham_column(0, 2, wei_a, orb_a, tile_a)
     for r in range(BLK_DEV):
         store(r, free, early_sem).start()
 
@@ -514,17 +536,19 @@
     vmem = pl.BlockSpec(memory_space=pltpu.VMEM)
     smem = pl.BlockSpec(memory_space=pltpu.SMEM)
     anywhere = pl.BlockSpec(memory_space=pl.ANY)
-    potential, orbitals, weighted, tiles, tiles_in = pl.pallas_call(
+    *held, tiles_in = pl.pallas_call(
         functools.partial(main_kernel, devices),
         out_shape=(
-            jax.ShapeDtypeStruct((SIDE, LAYER), f32),
+            pltpu.VMEM((SIDE, LAYER), f32),
             pltpu.VMEM((KB * FB, CELLS), bf16),
             pltpu.VMEM((NEAR * FB, CELLS), bf16),
             pltpu.VMEM((BOTH * FB, KB * FB), f32),
+            pltpu.VMEM((PAIR, PAIR), f32),
+            pltpu.VMEM((ROWS + FB, COLS), f32),
             jax.ShapeDtypeStruct((NEAR * FB, KB * FB), f32),
         ),
         in_specs=[smem, anywhere] + [vmem] * 4,
-        out_specs=(vmem, vmem, vmem, vmem, anywhere),
+        out_specs=(vmem,) * 6 + (anywhere,),
         scratch_shapes=[
             pltpu.VMEM((BLK_DEV, 5 * BLK_DEV, FB, FB), bf16),
             pltpu.VMEM((KB * FB, CELLS), bf16),
@@ -549,31 +573,38 @@
             pltpu.SemaphoreType.DMA((5,)),
             pltpu.SemaphoreType.DMA((5,)),
             pltpu.SemaphoreType.DMA((2,)),
-            pltpu.SemaphoreType.DMA((4,)),
-            pltpu.SemaphoreType.DMA((4,)),
+            pltpu.SemaphoreType.DMA((2,)),
+            pltpu.SemaphoreType.DMA((2,)),
         ],
         compiler_params=pltpu.CompilerParams(collective_id=0, has_side_effects=True, vmem_limit_bytes=VMEM_BYTES),
         name="build_tiles",
     )(blocks, density_rows.reshape(BLK_DEV, FB, COLS), *params)
-    held = [pltpu.with_memory_space_constraint(x, pltpu.VMEM) for x in (orbitals, weighted, tiles)]
-    return pl.pallas_call(
+    held = [pltpu.with_memory_space_constraint(x, pltpu.VMEM) for x in held]
+    potential, ham, _ = pl.pallas_call(
         functools.partial(out_kernel, devices),
-        out_shape=(jax.ShapeDtypeStruct((1, CELLS), f32), jax.ShapeDtypeStruct((ROWS, COLS), f32)),
-        in_specs=[smem] + [vmem] * 4 + [anywhere],
-        out_specs=(vmem, anywhere),
+        out_shape=(
+            jax.ShapeDtypeStruct((1, CELLS), f32),
+            jax.ShapeDtypeStruct((ROWS, COLS), f32),
+            pltpu.VMEM((ROWS + FB, COLS), f32),
+        ),
+        in_specs=[anywhere] + [vmem] * 6 + [anywhere],
+        out_specs=(vmem, anywhere, vmem),
+        input_output_aliases={6: 2},
         scratch_shapes=[
-            pltpu.VMEM((ROWS + FB, COLS), f32),
             pltpu.VMEM((NEAR * FB, KB * FB), f32),
             pltpu.VMEM((NEAR * FB, KB * FB), f32),
+            pltpu.SMEM((KB, devices), jnp.int32),
             pltpu.SMEM((3, KB), jnp.int32),
             pltpu.SMEM((3, KB), jnp.int32),
+            pltpu.SemaphoreType.DMA,
             pltpu.SemaphoreType.DMA,
             pltpu.SemaphoreType.DMA((BLK_DEV,)),
             pltpu.SemaphoreType.DMA((BLK_DEV,)),
         ],
         compiler_params=pltpu.CompilerParams(vmem_limit_bytes=VMEM_BYTES),
         name="place_tiles",
-    )(blocks, potential, *held, tiles_in)
+    )(blocks, *held, tiles_in)
+    return potential, ham
 
 
 def solution(mesh):

time: 46.8 us -> 43 us (0.919)
  Pallas kernels: 45.8 us -> 42.1 us
    pallas_call x1, Pallas kernels: 37 us -> 33.9 us  [local(): pl.pallas_call(functools.partial(main_kernel, devices), out_shape=(pltpu....]
    pallas_call x1, Pallas kernels: 8.77 us -> 8.17 us  [local(): pl.pallas_call(functools.partial(out_kernel, devices), out_shape=(jax.Sha...]
where the time goes in v3:
time: 43 us; the launch traced here: 42.9 us
  Pallas kernels  42.1 us (98%)
  between operations  0.8 us (2%)
    pallas_call x1, Pallas kernels, local(): pl.pallas_call(functools.partial(main_kernel, devices), out_shape=(pltpu....  33.9 us
    pallas_call x1, Pallas kernels, local(): pl.pallas_call(functools.partial(out_kernel, devices), out_shape=(jax.Sha...  8.17 us

profile of v3, /device:TPU:0, one launch (start us, length us, event | category | flops | bytes accessed | tf_op | source)
XLA Modules:
  0.0 42.9 jit_solution(5540225223680923067)
XLA Ops:
  0.6 33.9 %build_tiles.1 = (f32[16,256]{1,0:T(8,128)S(1)}, bf16[1024,4096]{1,0:T(8,128)(2,1)S(1)}, bf16[512,4096]{1,0:T(8,128)(2,1)S(1)}, f32[768,1024]{1,0:T(8,128)S(1)},...) custom-call(s32[8,32]{1,0:T(8,128)} %bitcast.11, bf16[6,128,3840]{2,1,0:T(8,128)(2,1)} %bitcast.6, ...), custom_call_target="tpu_custom_call" | custom-call | tf_op jit(solution)/shard_map/build_tiles/pallas_call | solution.py:539
  34.6 8.2 %place_tiles.1 = (f32[1,4096]{1,0:T(1,128)}, f32[768,3840]{1,0:T(8,128)}, f32[896,3840]{1,0:T(8,128)S(1)}) custom-call(s32[8,32]{1,0:T(8,128)} %bitcast.12, f32[16,256]{1,0:T(8,128)S(1)} %get-tuple-element.11.pot_in, bf16[1024,4096]{1,0:T(8,128)(2,1)S(1)} %get-tuple-element.12.orb_a, ...), custom_call_target="tpu_custom_call", output_to_operand_aliasing={{2}: (6, {})} | custom-call | tf_op jit(solution)/shard_map/place_tiles/pallas_call | solution.py:583

commit v4 on v3

--- a/solution.py
+++ b/solution.py
@@ -45,7 +45,7 @@
 )
 
 
-def order_blocks(which, brick, first, second, me, devices, bb_ref, slot_ref, col_ref):
+def order_blocks(which, brick, first, second, me, devices, bb_ref, slot_ref):
     keys = []
     for j in range(KB):
         block = bb_ref[j, brick]
@@ -62,7 +62,7 @@
         step = owner - me + 2
         step = jnp.where(step < 0, step + devices, jnp.where(step >= devices, step - devices, step))
         slot_ref[which, s] = owner * BLK_DEV + local
-        col_ref[which, s] = jnp.minimum(step, 4) * BLK_DEV + local
+        slot_ref[3 + which, s] = jnp.minimum(step, 4) * BLK_DEV + local
 
 
 def pair_of(me):
@@ -215,6 +215,7 @@
     corner,
     acc_ref,
     tiles_hbm,
+    lists_hbm,
     rows_vmem,
     orb_b,
     mat_a,
@@ -232,7 +233,6 @@
     after_in,
     sums,
     slot_ref,
-    col_ref,
     load_sem,
     mat_sem,
     send_sem,
@@ -240,6 +240,7 @@
     all_sem,
     tile_send,
     tile_recv,
+    list_sem,
 ):
     me = lax.axis_index("dev")
     odd = lax.rem(me, 2)
@@ -264,8 +265,10 @@
 
     lists = ((across, me, me), (me, pair, me), (pair, me, pair))
     for which, (brick, first, second) in enumerate(lists):
-        order_blocks(which, brick, first, second, me, devices, bb_ref, slot_ref, col_ref)
-
+        order_blocks(which, brick, first, second, me, devices, bb_ref, slot_ref)
+
+    keep_lists = pltpu.make_async_copy(slot_ref, lists_hbm, list_sem)
+    keep_lists.start()
     params = (cx, cy, cz, ex)
     spread_matrix(spread_ref)
 
@@ -285,7 +288,7 @@
         here = slice(a * FB, (a + 1) * FB)
         for c in range(0, KB, 2):
             there = slice(c * FB, (c + 2) * FB)
-            tiles = [rows_vmem[row, col_ref[which, c + h]] for h in range(2)]
+            tiles = [rows_vmem[row, slot_ref[3 + which, c + h]] for h in range(2)]
             tile = jnp.concatenate(tiles, axis=1) * mask
             target[here, there] = tile if other is None else tile + other[here, there]
 
@@ -389,7 +392,7 @@
         weigh_block(k, orb_b, pot_ref, 1 - odd, wei_b)
         return carry
 
-    lax.fori_loop(0, BOTH, weigh_b, 0)
+    lax.fori_loop(0, NEAR, weigh_b, 0)
 
     def give_tiles(n, cells):
         return pltpu.make_async_remote_copy(
@@ -404,6 +407,7 @@
     gives = [give_tiles(n, pl.ds(n * 2 * PAIR, 2 * PAIR)) for n in range(2)]
     for j in (3, 2):
         ham_column(j, 2, wei_b, orb_b, tile_b)
+        weigh_b(NEAR + 3 - j, 0)
         weigh_a(3 - j, 0)
     gives[1].start()
     for j in (1, 0):
@@ -421,11 +425,12 @@
     pltpu.make_async_copy(sums, sums, all_sem.at[0]).wait()
     for copy in gives:
         copy.wait()
+    keep_lists.wait()
 
 
 def out_kernel(
     devices,
-    bb_hbm,
+    lists_hbm,
     pot_in,
     orb_a,
     wei_a,
@@ -438,18 +443,14 @@
     acc_ref,
     tile_a,
     tile_in,
-    bb_ref,
     slot_ref,
-    col_ref,
     in_sem,
-    bb_sem,
+    list_sem,
     early_sem,
     late_sem,
 ):
     me = lax.axis_index("dev")
-    pair = pair_of(me)
-    across = across_of(me, devices)
-    lay = pltpu.make_async_copy(bb_hbm, bb_ref, bb_sem)
+    lay = pltpu.make_async_copy(lists_hbm, slot_ref, list_sem)
     lay.start()
     fetch = pltpu.make_async_copy(tiles_hbm, tile_in, in_sem)
     fetch.start()
@@ -457,9 +458,6 @@
         pot_out[:, i * LAYER : (i + 1) * LAYER] = pot_in[i : i + 1, :]
     tile_a[0:PAIR, 0:PAIR] = corner[...]
     lay.wait()
-    lists = ((across, me, me), (me, pair, me), (pair, me, pair))
-    for which, (brick, first, second) in enumerate(lists):
-        order_blocks(which, brick, first, second, me, devices, bb_ref, slot_ref, col_ref)
     sources = (tile_a, tile_b, tile_in)
     first_slot = (0, 2, 0)
 
@@ -469,7 +467,7 @@
         return owner == me, block - owner * BLK_DEV
 
     def tile_of(ref, row, which, c):
-        col = pl.multiple_of(col_ref[which, c] * FB, FB)
+        col = pl.multiple_of(slot_ref[3 + which, c] * FB, FB)
         return ref.at[pl.ds(pl.multiple_of(row * FB, FB), FB), pl.ds(col, FB)]
 
     def add(which):
@@ -484,20 +482,6 @@
         sum((slot_ref[0, s] == me * BLK_DEV + r).astype(jnp.int32) for s in range(CAP)) > 0 for r in range(BLK_DEV)
     ]
 
-    def store_row(r):
-        here = pl.ds(r * FB, FB)
-        return pltpu.make_async_copy(acc_ref.at[here], ham_hbm.at[here], early_sem.at[r])
-
-    def each_tile(act):
-        for s in range(CAP):
-            mine, row = owned(0, s)
-
-            @pl.when(mine)
-            def _():
-                for c in range(KB):
-                    source, target = tile_of(acc_ref, row, 0, c), tile_of(ham_hbm, row, 0, c)
-                    act(pltpu.make_async_copy(source, target, late_sem.at[s, c]))
-
     odd = lax.rem(me, 2)
     free = pl.ds(pl.multiple_of((1 - odd) * 3 * ROWS, FB), 2 * ROWS)
     shared = pl.ds(pl.multiple_of(odd * 2 * ROWS, FB), 3 * ROWS)
@@ -506,10 +490,21 @@
         here = pl.ds(r * FB, FB)
         return pltpu.make_async_copy(acc_ref.at[here, cols], ham_hbm.at[here, cols], sem.at[r])
 
-    add(1)
+    def add_row(which, r):
+        place = sum(
+            jnp.where(slot_ref[which, first_slot[which] + s] == me * BLK_DEV + r, s + 1, 0) for s in range(CAP)
+        )
+
+        @pl.when(place > 0)
+        def _():
+            start = pl.ds(pl.multiple_of((first_slot[which] + place - 1) * FB, FB), FB)
+            for c in range(KB):
+                tile_of(acc_ref, r, which, c)[...] += sources[which][start, c * FB : (c + 1) * FB]
+
     fetch.wait()
-    add(2)
     for r in range(BLK_DEV):
+        add_row(1, r)
+        add_row(2, r)
         store(r, free, early_sem).start()
 
         @pl.when(jnp.logical_not(across_rows[r]))
@@ -536,7 +531,7 @@
     vmem = pl.BlockSpec(memory_space=pltpu.VMEM)
     smem = pl.BlockSpec(memory_space=pltpu.SMEM)
     anywhere = pl.BlockSpec(memory_space=pl.ANY)
-    *held, tiles_in = pl.pallas_call(
+    *held, tiles_in, lists = pl.pallas_call(
         functools.partial(main_kernel, devices),
         out_shape=(
             pltpu.VMEM((SIDE, LAYER), f32),
@@ -546,9 +541,10 @@
             pltpu.VMEM((PAIR, PAIR), f32),
             pltpu.VMEM((ROWS + FB, COLS), f32),
             jax.ShapeDtypeStruct((NEAR * FB, KB * FB), f32),
+            jax.ShapeDtypeStruct((8, FB), jnp.int32),
         ),
         in_specs=[smem, anywhere] + [vmem] * 4,
-        out_specs=(vmem,) * 6 + (anywhere,),
+        out_specs=(vmem,) * 6 + (anywhere,) * 2,
         scratch_shapes=[
             pltpu.VMEM((BLK_DEV, 5 * BLK_DEV, FB, FB), bf16),
             pltpu.VMEM((KB * FB, CELLS), bf16),
@@ -566,8 +562,7 @@
             pltpu.VMEM((2, 8, LAYER), f32),
             pltpu.VMEM((2, 8, LAYER), f32),
             pltpu.VMEM((devices - 1, 1, FB), f32),
-            pltpu.SMEM((3, KB), jnp.int32),
-            pltpu.SMEM((3, KB), jnp.int32),
+            pltpu.SMEM((8, FB), jnp.int32),
             pltpu.SemaphoreType.DMA,
             pltpu.SemaphoreType.DMA((2,)),
             pltpu.SemaphoreType.DMA((5,)),
@@ -575,6 +570,7 @@
             pltpu.SemaphoreType.DMA((2,)),
             pltpu.SemaphoreType.DMA((2,)),
             pltpu.SemaphoreType.DMA((2,)),
+            pltpu.SemaphoreType.DMA,
         ],
         compiler_params=pltpu.CompilerParams(collective_id=0, has_side_effects=True, vmem_limit_bytes=VMEM_BYTES),
         name="build_tiles",
@@ -593,9 +589,7 @@
         scratch_shapes=[
             pltpu.VMEM((NEAR * FB, KB * FB), f32),
             pltpu.VMEM((NEAR * FB, KB * FB), f32),
-            pltpu.SMEM((KB, devices), jnp.int32),
-            pltpu.SMEM((3, KB), jnp.int32),
-            pltpu.SMEM((3, KB), jnp.int32),
+            pltpu.SMEM((8, FB), jnp.int32),
             pltpu.SemaphoreType.DMA,
             pltpu.SemaphoreType.DMA,
             pltpu.SemaphoreType.DMA((BLK_DEV,)),
@@ -603,7 +597,7 @@
         ],
         compiler_params=pltpu.CompilerParams(vmem_limit_bytes=VMEM_BYTES),
         name="place_tiles",
-    )(blocks, *held, tiles_in)
+    )(lists, *held, tiles_in)
     return potential, ham
 
 

time: 43 us -> 43.4 us (level)
  Pallas kernels: 42.1 us -> 42.7 us
    pallas_call x1, Pallas kernels: 8.17 us -> 8.89 us  [local(): pl.pallas_call(functools.partial(out_kernel, devices), out_shape=(jax.Sha...]
where the time goes in v4:
time: 43.4 us; the launch traced here: 43.5 us
  Pallas kernels  42.7 us (98%)
  between operations  0.8 us (2%)
    pallas_call x1, Pallas kernels, local(): pl.pallas_call(functools.partial(main_kernel, devices), out_shape=(pltpu....  33.8 us
    pallas_call x1, Pallas kernels, local(): pl.pallas_call(functools.partial(out_kernel, devices), out_shape=(jax.Sha...  8.89 us

profile of v4, /device:TPU:0, one launch (start us, length us, event | category | flops | bytes accessed | tf_op | source)
XLA Modules:
  0.0 43.5 jit_solution(8268878570836994304)
XLA Ops:
  0.6 33.8 %build_tiles.1 = (f32[16,256]{1,0:T(8,128)S(1)}, bf16[1024,4096]{1,0:T(8,128)(2,1)S(1)}, bf16[512,4096]{1,0:T(8,128)(2,1)S(1)}, f32[768,1024]{1,0:T(8,128)S(1)},...) custom-call(s32[8,32]{1,0:T(8,128)} %bitcast.11, ...), custom_call_target="tpu_custom_call" | custom-call | tf_op jit(solution)/shard_map/build_tiles/pallas_call | solution.py:534
  34.5 8.9 %place_tiles.1 = (f32[1,4096]{1,0:T(1,128)}, f32[768,3840]{1,0:T(8,128)}, f32[896,3840]{1,0:T(8,128)S(1)}) custom-call(s32[8,128]{1,0:T(8,128)} %get-tuple-element.12.lists_hbm, f32[16,256]{1,0:T(8,128)S(1)} %get-tuple-element.13.pot_in, bf16[1024,4096]{1,0:T(8,128)(2,1)S(1)} %get-tuple-element.14.orb_a, ...), custom_call_target="tpu_custom_call", output_to_operand_aliasing={{2}: (6, {})} | custom-call | tf_op jit(solution)/shard_map/place_tiles/pallas_call | solution.py:579

commit v5 on v4

--- a/solution.py
+++ b/solution.py
@@ -448,6 +448,7 @@
     list_sem,
     early_sem,
     late_sem,
+    last_sem,
 ):
     me = lax.axis_index("dev")
     lay = pltpu.make_async_copy(lists_hbm, slot_ref, list_sem)
@@ -470,13 +471,16 @@
         col = pl.multiple_of(slot_ref[3 + which, c] * FB, FB)
         return ref.at[pl.ds(pl.multiple_of(row * FB, FB), FB), pl.ds(col, FB)]
 
+    def add_slot(which, s):
+        mine, row = owned(which, s)
+        row = jnp.where(mine, row, BLK_DEV)
+        start = (first_slot[which] + s) * FB
+        for c in range(KB):
+            tile_of(acc_ref, row, which, c)[...] += sources[which][start : start + FB, c * FB : (c + 1) * FB]
+
     def add(which):
         for s in range(CAP):
-            mine, row = owned(which, s)
-            row = jnp.where(mine, row, BLK_DEV)
-            start = (first_slot[which] + s) * FB
-            for c in range(KB):
-                tile_of(acc_ref, row, which, c)[...] += sources[which][start : start + FB, c * FB : (c + 1) * FB]
+            add_slot(which, s)
 
     across_rows = [
         sum((slot_ref[0, s] == me * BLK_DEV + r).astype(jnp.int32) for s in range(CAP)) > 0 for r in range(BLK_DEV)
@@ -490,21 +494,10 @@
         here = pl.ds(r * FB, FB)
         return pltpu.make_async_copy(acc_ref.at[here, cols], ham_hbm.at[here, cols], sem.at[r])
 
-    def add_row(which, r):
-        place = sum(
-            jnp.where(slot_ref[which, first_slot[which] + s] == me * BLK_DEV + r, s + 1, 0) for s in range(CAP)
-        )
-
-        @pl.when(place > 0)
-        def _():
-            start = pl.ds(pl.multiple_of((first_slot[which] + place - 1) * FB, FB), FB)
-            for c in range(KB):
-                tile_of(acc_ref, r, which, c)[...] += sources[which][start, c * FB : (c + 1) * FB]
-
+    add(1)
     fetch.wait()
+    add(2)
     for r in range(BLK_DEV):
-        add_row(1, r)
-        add_row(2, r)
         store(r, free, early_sem).start()
 
         @pl.when(jnp.logical_not(across_rows[r]))
@@ -513,16 +506,26 @@
 
     for j in range(1, 4):
         ham_column(j, 2, wei_a, orb_a, tile_a)
-    add(0)
-    for r in range(BLK_DEV):
-
-        @pl.when(across_rows[r])
+    def store_slot(s, act):
+        mine, row = owned(0, s)
+
+        @pl.when(mine)
         def _():
-            store(r, shared, late_sem).start()
-
+            here = pl.ds(pl.multiple_of(row * FB, FB), FB)
+            act(pltpu.make_async_copy(acc_ref.at[here, shared], ham_hbm.at[here, shared], last_sem.at[s]))
+
+    for s in range(CAP):
+        add_slot(0, s)
+        store_slot(s, lambda copy: copy.start())
     for r in range(BLK_DEV):
         store(r, free, early_sem).wait()
-        store(r, shared, late_sem).wait()
+
+        @pl.when(jnp.logical_not(across_rows[r]))
+        def _():
+            store(r, shared, late_sem).wait()
+
+    for s in range(CAP):
+        store_slot(s, lambda copy: copy.wait())
 
 
 def local(devices, density_rows, center_x, center_y, center_z, exponent, brick_blocks):
@@ -594,6 +597,7 @@
             pltpu.SemaphoreType.DMA,
             pltpu.SemaphoreType.DMA((BLK_DEV,)),
             pltpu.SemaphoreType.DMA((BLK_DEV,)),
+            pltpu.SemaphoreType.DMA((CAP,)),
         ],
         compiler_params=pltpu.CompilerParams(vmem_limit_bytes=VMEM_BYTES),
         name="place_tiles",

time: 43.4 us -> 43 us (level)
  Pallas kernels: 42.7 us -> 42 us
    pallas_call x1, Pallas kernels: 8.89 us -> 8 us  [local(): pl.pallas_call(functools.partial(out_kernel, devices), out_shape=(jax.Sha...]
where the time goes in v5:
time: 43 us; the launch traced here: 42.8 us
  Pallas kernels  42 us (98%)
  between operations  0.8 us (2%)
    pallas_call x1, Pallas kernels, local(): pl.pallas_call(functools.partial(main_kernel, devices), out_shape=(pltpu....  34 us
    pallas_call x1, Pallas kernels, local(): pl.pallas_call(functools.partial(out_kernel, devices), out_shape=(jax.Sha...  8 us

profile of v5, /device:TPU:0, one launch (start us, length us, event | category | flops | bytes accessed | tf_op | source)
XLA Modules:
  0.0 42.8 jit_solution(11382531560106439578)
XLA Ops:
  0.6 34.0 %build_tiles.1 = (f32[16,256]{1,0:T(8,128)S(1)}, bf16[1024,4096]{1,0:T(8,128)(2,1)S(1)}, bf16[512,4096]{1,0:T(8,128)(2,1)S(1)}, f32[768,1024]{1,0:T(8,128)S(1)},...) custom-call(s32[8,32]{1,0:T(8,128)} %bitcast.11, ...), custom_call_target="tpu_custom_call" | custom-call | tf_op jit(solution)/shard_map/build_tiles/pallas_call | solution.py:537
  34.6 8.0 %place_tiles.1 = (f32[1,4096]{1,0:T(1,128)}, f32[768,3840]{1,0:T(8,128)}, f32[896,3840]{1,0:T(8,128)S(1)}) custom-call(s32[8,128]{1,0:T(8,128)} %get-tuple-element.12.lists_hbm, f32[16,256]{1,0:T(8,128)S(1)} %get-tuple-element.13.pot_in, bf16[1024,4096]{1,0:T(8,128)(2,1)S(1)} %get-tuple-element.14.orb_a, ...), custom_call_target="tpu_custom_call", output_to_operand_aliasing={{2}: (6, {})} | custom-call | tf_op jit(solution)/shard_map/place_tiles/pallas_call | solution.py:582
